TPU v7x, 128 devices: a whole 4x4x4 slice. The times are simulated.
128 devices in a mesh: cuts: 2 (over x_hi), section: 4 (over y), dp: 16 (over z, x_lo, core).
Axes of the slice: x: 4 (x_hi: 2, x_lo: 2; x = x_hi * 2 + x_lo), y: 4, z: 4, core: 2. Of those that a mesh axis runs over, the one named last changes fastest.
Arguments:
- activations: bfloat16 [2, 4, 4096, 4096], P('cuts', 'section', 'dp'), may hold values from -6 to 6
- upstream_grad: bfloat16 [2, 4, 4096, 4096], P('cuts', 'section', 'dp'), may hold values from -6 to 6
- routes: int32 [2, 4, 4096, 4], P('cuts', 'section', 'dp'), may hold values from 0 to 15, as said below
- router_probs: float32 [2, 4, 4096, 4], P('cuts', 'section', 'dp'), may hold values from 0.2 to 1
- gate_weight: bfloat16 [4, 5376, 4096], P('section', 'dp'), may hold values from -0.09375 to 0.09375
- up_weight: bfloat16 [4, 5376, 4096], P('section', 'dp'), may hold values from -0.09375 to 0.09375
- down_weight: bfloat16 [4, 5376, 4096], P('section', 'dp'), may hold values from -0.078125 to 0.078125
Outputs:
- grad_gate: bfloat16 [4, 5376, 4096], P('section', 'dp')
- grad_up: bfloat16 [4, 5376, 4096], P('section', 'dp')
- grad_down: bfloat16 [4, 5376, 4096], P('section', 'dp')
- prev_grad: bfloat16 [2, 4, 4096, 4096], P('cuts', 'section', 'dp')
Inputs may be any that keep to these rules, and one draw needn't show every extreme that they name: `routes`: each token names 4 different experts. In every aligned block of 256 tokens of one replica and section, from 32 to 64 tokens name expert 0, and in every draw some block has exactly 64.
All inputs are finite; a program needn't handle non-finite values.
Results may differ from a plain program's by a relative error of at most 0.025.
Values may be sent and summed in bfloat16 or wider, within the bound.
No kernel may reach another device: no remote copies, remote signals or barrier semaphores. Data moves between devices by JAX's collectives and lax.ppermute only.
A program may use at most 192 MiB of HBM per device.

v0:
```python
import jax
import jax.numpy as jnp
from jax import lax
from jax.sharding import PartitionSpec as P

CAP = 64


def from_behind(block, axis, distance):
    devices = range(lax.axis_size(axis))
    route = [(i - distance, i) for i in devices if i - distance in devices]
    return lax.ppermute(block, axis, route)


def contract_last(left, right):
    return lax.dot_general(
        left, right, (((1,), (1,)), ((), ())), preferred_element_type=jnp.float32
    )


def contract_first(left, right):
    return lax.dot_general(
        left, right, (((0,), (0,)), ((), ())), preferred_element_type=jnp.float32
    )


def per_device(
    activations, upstream_grad, routes, router_probs, gate_weight, up_weight, down_weight
):
    local_acts = activations[0, 0]
    local_grads = upstream_grad[0, 0]
    expert_hits = routes[0, 0] == 0
    router_weight = jnp.sum(jnp.where(expert_hits, router_probs[0, 0], jnp.float32(0.0)), axis=1)
    is_routed = jnp.any(expert_hits, axis=1)
    row_index = jnp.cumsum(is_routed.astype(jnp.int32)) - 1
    wanted = jnp.arange(CAP, dtype=jnp.int32)
    picker = ((row_index[None, :] == wanted[:, None]) & is_routed[None, :]).astype(jnp.bfloat16)
    scaled = (router_weight[:, None] * local_grads.astype(jnp.float32)).astype(jnp.bfloat16)
    packed_acts = jnp.dot(picker, local_acts, preferred_element_type=jnp.float32).astype(
        jnp.bfloat16
    )
    packed_grads = jnp.dot(picker, scaled, preferred_element_type=jnp.float32).astype(jnp.bfloat16)
    rows_acts, rows_grads = (
        lax.all_gather(packed_acts, "dp", axis=0, tiled=True),
        lax.all_gather(packed_grads, "dp", axis=0, tiled=True),
    )
    gate_local = gate_weight[0]
    up_local = up_weight[0]
    down_local = down_weight[0]
    gate_pre = contract_last(rows_acts, gate_local)
    up_pre = contract_last(rows_acts, up_local)
    sig_gate = jax.nn.sigmoid(gate_pre)
    silu_gate = gate_pre * sig_gate
    hidden = (silu_gate * up_pre).astype(jnp.bfloat16)
    hidden_grad = contract_last(rows_grads, down_local)
    gate_grad = (hidden_grad * up_pre * sig_gate * (1.0 + gate_pre * (1.0 - sig_gate))).astype(
        jnp.bfloat16
    )
    up_grad = (hidden_grad * silu_gate).astype(jnp.bfloat16)
    down_part = contract_first(hidden, rows_grads)
    gate_part = contract_first(gate_grad, rows_acts)
    up_part = contract_first(up_grad, rows_acts)
    gate_total, up_total, down_total = (
        lax.psum(gate_part.astype(jnp.bfloat16), "cuts").astype(jnp.float32),
        lax.psum(up_part.astype(jnp.bfloat16), "cuts").astype(jnp.float32),
        lax.psum(down_part.astype(jnp.bfloat16), "cuts").astype(jnp.float32),
    )
    input_rows = lax.psum_scatter(
        (
            jnp.dot(gate_grad, gate_local, preferred_element_type=jnp.float32)
            + jnp.dot(up_grad, up_local, preferred_element_type=jnp.float32)
        ).astype(jnp.bfloat16),
        "dp",
        scatter_dimension=0,
        tiled=True,
    )
    token_grad = contract_first(picker, input_rows).astype(jnp.bfloat16)
    prev_grad = from_behind(token_grad[None, None], "section", -1)
    grad_gate = gate_total.astype(jnp.bfloat16)[None]
    grad_up = up_total.astype(jnp.bfloat16)[None]
    grad_down = down_total.astype(jnp.bfloat16)[None]
    return (grad_gate, grad_up, grad_down, prev_grad)


def solution(mesh):
    placed = (
        P("cuts", "section", "dp", None),
        P("cuts", "section", "dp", None),
        P("cuts", "section", "dp", None),
        P("cuts", "section", "dp", None),
        P("section", "dp", None),
        P("section", "dp", None),
        P("section", "dp", None),
    )
    return jax.shard_map(
        per_device,
        mesh=mesh,
        in_specs=placed,
        out_specs=(
            P("section", "dp", None),
            P("section", "dp", None),
            P("section", "dp", None),
            P("cuts", "section", "dp", None),
        ),
        check_vma=False,
    )
```

profile of v0, /device:TPU:1, one launch (start us, length us, event | category | flops | bytes accessed | tf_op | source)
XLA Modules:
  0.0 471.8 jit_solution(16867495214857487981)
XLA Ops:
  7.2 0.0 all-gather.5.cloned.1.call-start
  7.2 0.9 select_reduce_fusion
  8.1 0.3 reduce-window.9
  8.4 0.1 slice.7
  8.6 0.1 slice_reduce_fusion
  8.7 0.1 add_bitcast_fusion
  8.7 2.9 convolution_convert_fusion.4
  11.6 0.0 all-gather.3.cloned.1.call-start
  11.7 3.0 convolution_convert_fusion.5
  14.7 0.0 reduce-scatter.2.cloned.1.call-start
  14.8 52.8 %all-gather.5.cloned.1.call-done = bf16[1024,4096]{1,0:T(8,128)(2,1)} async-done(((bf16[64,4096]{1,0:T(8,128)(2,1)}), bf16[1024,4096]{1,0:T(8,128)(2,1)}) %all-gather.5.cloned.1.call-update) | async-done | bytes 8388624 | tf_op jit(solution)/shard_map/all_gather | solution.py:44
  67.6 7.6 %fusion.7 = f32[1024,336]{0,1:T(8,128)} fusion(bf16[1024,4096]{1,0:T(8,128)(2,1)} %all-gather.5.cloned.1.call-done, bf16[1,336,4096]{2,1,0:T(8,128)(2,1)S(1)} %copy-done), kind=kOutput, calls=%fused_computation.15 | convolution fusion | flops 2818572288 | bytes 12517376 | tf_op jit(solution)/shard_map/dot_general | solution.py:16
  75.2 4.1 fusion.10
  79.3 43.7 %all-gather.3.cloned.1.call-done = bf16[1024,4096]{1,0:T(8,128)(2,1)} async-done(((bf16[64,4096]{1,0:T(8,128)(2,1)}), bf16[1024,4096]{1,0:T(8,128)(2,1)}) %all-gather.3.cloned.1.call-update) | async-done | bytes 8388624 | tf_op jit(solution)/shard_map/all_gather | solution.py:45
  123.0 8.3 %multiply_convert_fusion.1 = (bf16[1024,336]{0,1:T(8,128)(2,1)S(1)}, bf16[1024,336]{0,1:T(8,128)(2,1)S(1)}) fusion(f32[1024,336]{0,1:T(8,128)} %fusion.7, f32[1024,336]{0,1:T(8,128)} %fusion.10, bf16[1024,4096]{1,0:T(8,128)(2,1)} %all-gather.3.cloned.1.call-done, bf16[1,336,4096]{2,1,0:T(8,128)(2,1)} %param.13), kind=kOutput, calls=%fused_computation.26 | convolution fusion | flops 2823045120 | bytes 15269888 | tf_op jit(solution)/shard_map/dot_general | solution.py:16
  131.4 8.3 %fusion.5 = f32[1024,4096]{1,0:T(8,128)} fusion(bf16[1024,336]{0,1:T(8,128)(2,1)S(1)} %get-tuple-element.10, bf16[1,336,4096]{2,1,0:T(8,128)(2,1)S(1)} %copy-done), kind=kOutput, calls=%fused_computation.13 | convolution fusion | flops 2818572288 | bytes 20217856 | tf_op jit(solution)/shard_map/dot_general | solution.py:70
  139.7 10.2 %add_convert_fusion = bf16[1024,4096]{1,0:T(8,128)(2,1)} fusion(f32[1024,4096]{1,0:T(8,128)} %fusion.5, bf16[1024,336]{0,1:T(8,128)(2,1)S(1)} %get-tuple-element.9, bf16[1,336,4096]{2,1,0:T(8,128)(2,1)S(1)} %copy-done.5), kind=kOutput, calls=%fused_computation | convolution fusion | flops 2826960896 | bytes 28606464 | tf_op jit(solution)/shard_map/dot_general | solution.py:71
  149.9 0.0 all-reduce.3.cloned.1.call-start
  150.0 7.8 %fusion.1 = bf16[1,336,4096]{2,1,0:T(8,128)(2,1)} fusion(bf16[1024,336]{0,1:T(8,128)(2,1)S(1)} %get-tuple-element.9, bf16[1024,4096]{1,0:T(8,128)(2,1)} %all-gather.5.cloned.1.call-done), kind=kOutput, calls=%fused_computation.6 | convolution fusion | flops 2819948544 | bytes 11829248 | tf_op jit(solution)/shard_map/dot_general | solution.py:22
  157.8 8.2 %fusion = bf16[1,336,4096]{2,1,0:T(8,128)(2,1)} fusion(bf16[1024,336]{0,1:T(8,128)(2,1)S(1)} %copy-done.9, bf16[1024,4096]{1,0:T(8,128)(2,1)} %all-gather.5.cloned.1.call-done), kind=kOutput, calls=%fused_computation.5 | convolution fusion | flops 2819948544 | bytes 11829248 | tf_op jit(solution)/shard_map/dot_general | solution.py:22
  166.1 4.5 fusion.2
  170.6 76.1 %reduce-scatter.2.cloned.1.call-done = bf16[64,4096]{1,0:T(8,128)(2,1)} async-done(((bf16[1024,4096]{1,0:T(8,128)(2,1)}), bf16[64,4096]{1,0:T(8,128)(2,1)}) %reduce-scatter.2.cloned.1.call-update) | async-done | bytes 524304 | tf_op jit(solution)/shard_map/reduce_scatter | solution.py:68
  246.7 1.8 fusion.3
  248.5 1.3 collective-permute-start
  249.8 45.3 %collective-permute-done = bf16[1,1,256,4096]{3,2,1,0:T(8,128)(2,1)S(1)} collective-permute-done((bf16[1,1,256,4096]{3,2,1,0:T(8,128)(2,1)S(1)}, bf16[1,1,256,4096]{3,2,1,0:T(8,128)(2,1)S(1)}, u32[]{:S(2)}, u32[]{:S(2)}) %collective-permute-start) | collective-permute-done | bytes 2097184 | tf_op jit(solution)/shard_map/ppermute | solution.py:12
  295.0 159.8 %all-reduce.3.cloned.1.call-done = (bf16[1,336,4096]{2,1,0:T(8,128)(2,1)}, bf16[1,336,4096]{2,1,0:T(8,128)(2,1)}, bf16[1,336,4096]{2,1,0:T(8,128)(2,1)}) async-done(((bf16[1,336,4096]{2,1,0:T(8,128)(2,1)}, bf16[1,336,4096]{2,1,0:T(8,128)(2,1)}, bf16[1,336,4096]{2,1,0:T(8,128)(2,1)}), (bf16[1,336,4096]{2,1,0:T(8,128)(2,1)}, bf16[1,336,4096]{2,1,0:T(8,128)(2,1)}, ...) | async-done | bytes 8257552 | tf_op jit(solution)/shard_map/psum | solution.py:64
  454.8 3.8 copy.15
  458.6 1.5 copy.16
  460.1 1.2 copy-done.2
  461.4 1.5 copy.17
  462.9 1.0 copy-done.7
  463.9 1.3 copy.18
  (36 shorter events, 0.2 us)
Async XLA Ops:
  7.2 60.4 %copy-start = (bf16[1,336,4096]{2,1,0:T(8,128)(2,1)S(1)}, bf16[1,336,4096]{2,1,0:T(8,128)(2,1)}, u32[]{:S(2)}) copy-start(bf16[1,336,4096]{2,1,0:T(8,128)(2,1)} %param.11) | copy-start | bytes 8257540
  7.2 60.4 %all-gather.5.cloned.1.call-start = ((), (), s32[]{:S(2)}) async-start(), calls=%async_computation.2 | async-start | bytes 8912896 | tf_op jit(solution)/shard_map/all_gather | solution.py:44
  11.6 111.4 %all-gather.3.cloned.1.call-start = ((), (), s32[]{:S(2)}) async-start(), calls=%async_computation.1 | async-start | bytes 8912896 | tf_op jit(solution)/shard_map/all_gather | solution.py:45
  14.7 232.0 %reduce-scatter.2.cloned.1.call-start = ((), (), s32[]{:S(2)}) async-start(), calls=%async_computation.3 | async-start | bytes 8912896 | tf_op jit(solution)/shard_map/reduce_scatter | solution.py:68
  67.6 7.7 %copy-start.4 = (bf16[1,336,4096]{2,1,0:T(8,128)(2,1)S(1)}, bf16[1,336,4096]{2,1,0:T(8,128)(2,1)}, u32[]{:S(2)}) copy-start(bf16[1,336,4096]{2,1,0:T(8,128)(2,1)} %param.12) | copy-start | bytes 8257540
  67.6 7.7 %copy-start.10 = (bf16[1024,4096]{1,0:T(8,128)(2,1)S(1)}, bf16[1024,4096]{1,0:T(8,128)(2,1)}, u32[]{:S(2)}) copy-start(bf16[1024,4096]{1,0:T(8,128)(2,1)} %all-gather.5.cloned.1.call-done) | copy-start | bytes 25165828
  131.4 8.3 %copy-start.8 = (bf16[1024,336]{0,1:T(8,128)(2,1)}, bf16[1024,336]{0,1:T(8,128)(2,1)S(1)}, u32[]{:S(2)}) copy-start(bf16[1024,336]{0,1:T(8,128)(2,1)S(1)} %get-tuple-element.10) | copy-start | bytes 2064388
  131.4 8.3 %copy-start.5 = (bf16[1,336,4096]{2,1,0:T(8,128)(2,1)S(1)}, bf16[1,336,4096]{2,1,0:T(8,128)(2,1)}, u32[]{:S(2)}) copy-start(bf16[1,336,4096]{2,1,0:T(8,128)(2,1)} %param.12) | copy-start | bytes 8257540
  149.9 7.9 %copy-start.9 = (bf16[1024,336]{0,1:T(8,128)(2,1)S(1)}, bf16[1024,336]{0,1:T(8,128)(2,1)}, u32[]{:S(2)}) copy-start(bf16[1024,336]{0,1:T(8,128)(2,1)} %copy-done.8) | copy-start | bytes 2064388
  149.9 304.9 %all-reduce.3.cloned.1.call-start = ((), (), s32[]{:S(2)}) async-start(), calls=%async_computation.4 | async-start | bytes 16515072 | tf_op jit(solution)/shard_map/psum | solution.py:64
  150.0 16.1 %slice-start = ((s8[8388608]{0:T(1024)(128)(4,1)}), s8[4194304]{0:T(1024)(128)(4,1)S(1)}, s32[]{:S(2)}) async-start(s8[8388608]{0:T(1024)(128)(4,1)} %bitcast.47), calls=%async_computation.5 | async-start | bytes 8388608
  157.8 8.3 %slice-start.1 = ((s8[8388608]{0:T(1024)(128)(4,1)}), s8[4194304]{0:T(1024)(128)(4,1)S(1)}, s32[]{:S(2)}) async-start(s8[8388608]{0:T(1024)(128)(4,1)} %bitcast.47), calls=%async_computation.6 | async-start | bytes 8388608
  157.8 8.3 %copy-start.11 = (f32[1024,336]{0,1:T(8,128)S(1)}, f32[1024,336]{0,1:T(8,128)}, u32[]{:S(2)}) copy-start(f32[1024,336]{0,1:T(8,128)} %fusion.7) | copy-start | bytes 4128772
  157.8 8.3 %copy-start.12 = (f32[1024,336]{0,1:T(8,128)S(1)}, f32[1024,336]{0,1:T(8,128)}, u32[]{:S(2)}) copy-start(f32[1024,336]{0,1:T(8,128)} %fusion.10) | copy-start | bytes 4128772
  248.5 46.6 %collective-permute-start = (bf16[1,1,256,4096]{3,2,1,0:T(8,128)(2,1)S(1)}, bf16[1,1,256,4096]{3,2,1,0:T(8,128)(2,1)S(1)}, u32[]{:S(2)}, u32[]{:S(2)}) collective-permute-start(bf16[1,1,256,4096]{3,2,1,0:T(8,128)(2,1)S(1)} %fusion.3), channel_id=1, source_target_pairs={{16,0},{32,16},{48,32},{17,1},{33,17},{49,33},{18,2},{34,18},{50,3... | collective-permute-start | bytes 6291464 | tf_op jit(solution)/shard_map/ppermute | solution.py:12
  295.0 159.8 %copy-start.6 = (bf16[1,1,256,4096]{3,2,1,0:T(8,128)(2,1)}, bf16[1,1,256,4096]{3,2,1,0:T(8,128)(2,1)S(1)}, u32[]{:S(2)}) copy-start(bf16[1,1,256,4096]{3,2,1,0:T(8,128)(2,1)S(1)} %collective-permute-done) | copy-start | bytes 6291460
  454.8 3.8 copy-start.3
  458.6 2.8 copy-start.2
  461.4 2.6 copy-start.7
  461.4 3.9 copy-start.1
Sparse Core Ops, SparseCore 0:
  11.8 55.7 all-gather.4
  69.9 53.1 all-gather.2
  150.0 96.6 reduce-scatter.1
  250.0 204.7 all-reduce.2
where the time goes:
time: 472 us
  waiting for transfers between devices  378 us (80%)
  matrix products  66.8 us (14%)
  between operations  13.9 us (3%)
  local copies, waits for them, and re-layouts  10.7 us (2%)
    psum x1, waiting for transfers between devices, per_device(): lax.psum(gate_part.astype(jnp.bfloat16), 'cuts').astype(jnp.float32)  160 us
    reduce_scatter x1, waiting for transfers between devices, per_device(): lax.psum_scatter((jnp.dot(gate_grad, gate_local, preferred_element_type=j...  76.1 us
    all_gather x1, waiting for transfers between devices, per_device(): lax.all_gather(packed_acts, 'dp', axis=0, tiled=True)  52.8 us
    ppermute x1, waiting for transfers between devices, from_behind(): return lax.ppermute(block, axis, route)  45.3 us
    all_gather x1, waiting for transfers between devices, per_device(): lax.all_gather(packed_grads, 'dp', axis=0, tiled=True)  43.7 us
    dot_general x4, matrix products, contract_first(): lax.dot_general(left, right, (((0,), (0,)), ((), ())), preferred_element_...  22.4 us
    dot_general x3, matrix products, contract_last(): lax.dot_general(left, right, (((1,), (1,)), ((), ())), preferred_element_...  20.1 us
    unnamed x34, local copies, waits for them, and re-layouts  10.5 us
  transfers between devices with their start and end apart: 5, of which 5 were waited for; matrix products, arithmetic and copies ran while one was open for 8% of the time, Pallas kernels for 0%

commit v1 on v0

--- a/solution.py
+++ b/solution.py
@@ -42,7 +42,9 @@
     packed_grads = jnp.dot(picker, scaled, preferred_element_type=jnp.float32).astype(jnp.bfloat16)
     rows_acts, rows_grads = (
         lax.all_gather(packed_acts, "dp", axis=0, tiled=True),
-        lax.all_gather(packed_grads, "dp", axis=0, tiled=True),
+        jnp.concatenate(
+            lax.all_to_all(jnp.stack([packed_grads] * lax.axis_size("dp")), "dp", 0, 0), axis=0
+        ),
     )
     gate_local = gate_weight[0]
     up_local = up_weight[0]

time: 472 us -> 531 us (1.12)
  waiting for transfers between devices: 378 us -> 421 us
  starting transfers between devices: 1.46 us -> 9.16 us
    all_gather x1, waiting for transfers between devices: 52.8 us -> 136 us  [per_device(): lax.all_gather(packed_acts, 'dp', axis=0, tiled=True)]
    all_gather x1 -> x0, waiting for transfers between devices: 43.7 us -> none  [per_device(): lax.all_gather(packed_grads, 'dp', axis=0, tiled=True)]
    all_to_all x0 -> x1, starting transfers between devices: none -> 7.76 us  [per_device(): lax.all_to_all(jnp.stack([packed_grads] * lax.axis_size('dp')), 'dp', 0, 0)]
  transfers between devices with their start and end apart: 5 -> 5, of which waited for: 5 -> 4; matrix products, arithmetic and copies ran while one was open for 8% -> 8% of each run, Pallas kernels for 0% -> 0%
where the time goes in v1:
time: 531 us; the launch traced here: 530 us
  waiting for transfers between devices  421 us (79%)
  matrix products  69.4 us (13%)
  local copies, waits for them, and re-layouts  15 us (3%)
  between operations  13.8 us (3%)
  starting transfers between devices  9.16 us (2%)
    psum x1, waiting for transfers between devices, per_device(): lax.psum(gate_part.astype(jnp.bfloat16), 'cuts').astype(jnp.float32)  160 us
    all_gather x1, waiting for transfers between devices, per_device(): lax.all_gather(packed_acts, 'dp', axis=0, tiled=True)  136 us
    reduce_scatter x1, waiting for transfers between devices, per_device(): lax.psum_scatter((jnp.dot(gate_grad, gate_local, preferred_element_type=j...  80 us
    ppermute x1, waiting for transfers between devices, from_behind(): return lax.ppermute(block, axis, route)  45.2 us
    dot_general x4, matrix products, contract_first(): lax.dot_general(left, right, (((0,), (0,)), ((), ())), preferred_element_...  25.6 us
    dot_general x3, matrix products, contract_last(): lax.dot_general(left, right, (((1,), (1,)), ((), ())), preferred_element_...  20.1 us
  transfers between devices with their start and end apart: 5, of which 4 were waited for; matrix products, arithmetic and copies ran while one was open for 8% of the time, Pallas kernels for 0%

profile of v1, /device:TPU:1, one launch (start us, length us, event | category | flops | bytes accessed | tf_op | source)
XLA Modules:
  0.0 530.1 jit_solution(6373671663273915872)
XLA Ops:
  7.2 0.0 all-gather.2.cloned.1.call-start
  7.2 0.9 select_reduce_fusion
  8.1 0.3 reduce-window.9
  8.4 0.1 slice.7
  8.6 0.1 slice_reduce_fusion
  8.7 0.1 add_bitcast_fusion
  8.7 2.9 convolution_convert_fusion.4
  11.6 2.2 convolution_convert_fusion.5
  13.8 4.3 stack.2
  18.1 7.8 %all-to-all-start = ((bf16[16,64,4096]{2,1,0:T(8,128)(2,1)}), bf16[16,64,4096]{2,1,0:T(8,128)(2,1)}, u32[]{:S(2)}, u32[]{:S(2)}) async-start(bf16[16,64,4096]{2,1,0:T(8,128)(2,1)} %stack.2), calls=%async_computation | async-start | bytes 16777216 | tf_op jit(solution)/shard_map/all_to_all | solution.py:46
  25.9 0.0 reduce-scatter.2.cloned.1.call-start
  25.9 136.2 %all-gather.2.cloned.1.call-done = bf16[1024,4096]{1,0:T(8,128)(2,1)} async-done(((bf16[64,4096]{1,0:T(8,128)(2,1)}), bf16[1024,4096]{1,0:T(8,128)(2,1)}) %all-gather.2.cloned.1.call-update) | async-done | bytes 8388624 | tf_op jit(solution)/shard_map/all_gather | solution.py:44
  162.1 7.6 %fusion.7 = f32[1024,336]{0,1:T(8,128)} fusion(bf16[1024,4096]{1,0:T(8,128)(2,1)} %all-gather.2.cloned.1.call-done, bf16[1,336,4096]{2,1,0:T(8,128)(2,1)S(1)} %copy-done), kind=kOutput, calls=%fused_computation.15 | convolution fusion | flops 2818572288 | bytes 12517376 | tf_op jit(solution)/shard_map/dot_general | solution.py:16
  169.7 4.1 fusion.10
  173.9 8.3 %multiply_convert_fusion.1 = (bf16[1024,336]{0,1:T(8,128)(2,1)S(1)}, bf16[1024,336]{0,1:T(8,128)(2,1)S(1)}) fusion(f32[1024,336]{0,1:T(8,128)} %fusion.7, f32[1024,336]{0,1:T(8,128)} %fusion.10, bf16[1024,4096]{1,0:T(8,128)(2,1)} %bitcast.3, bf16[1,336,4096]{2,1,0:T(8,128)(2,1)} %param.13), kind=kOutput, calls=%fused_computation.26 | convolution fusion | flops 2823045120 | bytes 15269888 | tf_op jit(solution)/shard_map/dot_general | solution.py:16
  182.2 8.4 %fusion.5 = f32[1024,4096]{1,0:T(8,128)} fusion(bf16[1024,336]{0,1:T(8,128)(2,1)S(1)} %get-tuple-element.10, bf16[1,336,4096]{2,1,0:T(8,128)(2,1)S(1)} %copy-done), kind=kOutput, calls=%fused_computation.13 | convolution fusion | flops 2818572288 | bytes 20217856 | tf_op jit(solution)/shard_map/dot_general | solution.py:72
  190.6 10.3 %add_convert_fusion = bf16[1024,4096]{1,0:T(8,128)(2,1)} fusion(f32[1024,4096]{1,0:T(8,128)} %fusion.5, bf16[1024,336]{0,1:T(8,128)(2,1)S(1)} %get-tuple-element.9, bf16[1,336,4096]{2,1,0:T(8,128)(2,1)S(1)} %copy-done.5), kind=kOutput, calls=%fused_computation | convolution fusion | flops 2826960896 | bytes 28606464 | tf_op jit(solution)/shard_map/dot_general | solution.py:73
  200.9 0.0 all-reduce.3.cloned.1.call-start
  201.0 7.7 %fusion.1 = bf16[1,336,4096]{2,1,0:T(8,128)(2,1)} fusion(bf16[1024,336]{0,1:T(8,128)(2,1)S(1)} %get-tuple-element.9, bf16[1024,4096]{1,0:T(8,128)(2,1)} %all-gather.2.cloned.1.call-done), kind=kOutput, calls=%fused_computation.6 | convolution fusion | flops 2819948544 | bytes 11829248 | tf_op jit(solution)/shard_map/dot_general | solution.py:22
  208.7 7.8 %fusion = bf16[1,336,4096]{2,1,0:T(8,128)(2,1)} fusion(bf16[1024,336]{0,1:T(8,128)(2,1)S(1)} %copy-done.9, bf16[1024,4096]{1,0:T(8,128)(2,1)} %all-gather.2.cloned.1.call-done), kind=kOutput, calls=%fused_computation.5 | convolution fusion | flops 2819948544 | bytes 11829248 | tf_op jit(solution)/shard_map/dot_general | solution.py:22
  216.6 8.2 %fusion.2 = bf16[1,336,4096]{2,1,0:T(8,128)(2,1)} fusion(bf16[1024,4096]{1,0:T(8,128)(2,1)} %bitcast.3, f32[1024,336]{0,1:T(8,128)S(1)} %copy-done.12, f32[1024,336]{0,1:T(8,128)S(1)} %copy-done.11), kind=kOutput, calls=%fused_computation.7 | convolution fusion | flops 2822012928 | bytes 13893632 | tf_op jit(solution)/shard_map/dot_general | solution.py:22
  224.8 80.0 %reduce-scatter.2.cloned.1.call-done = bf16[64,4096]{1,0:T(8,128)(2,1)} async-done(((bf16[1024,4096]{1,0:T(8,128)(2,1)}), bf16[64,4096]{1,0:T(8,128)(2,1)}) %reduce-scatter.2.cloned.1.call-update) | async-done | bytes 524304 | tf_op jit(solution)/shard_map/reduce_scatter | solution.py:70
  304.9 1.8 fusion.3
  306.6 1.3 collective-permute-start
  307.9 45.2 %collective-permute-done = bf16[1,1,256,4096]{3,2,1,0:T(8,128)(2,1)S(1)} collective-permute-done((bf16[1,1,256,4096]{3,2,1,0:T(8,128)(2,1)S(1)}, bf16[1,1,256,4096]{3,2,1,0:T(8,128)(2,1)S(1)}, u32[]{:S(2)}, u32[]{:S(2)}) %collective-permute-start) | collective-permute-done | bytes 2097184 | tf_op jit(solution)/shard_map/ppermute | solution.py:12
  353.2 159.9 %all-reduce.3.cloned.1.call-done = (bf16[1,336,4096]{2,1,0:T(8,128)(2,1)}, bf16[1,336,4096]{2,1,0:T(8,128)(2,1)}, bf16[1,336,4096]{2,1,0:T(8,128)(2,1)}) async-done(((bf16[1,336,4096]{2,1,0:T(8,128)(2,1)}, bf16[1,336,4096]{2,1,0:T(8,128)(2,1)}, bf16[1,336,4096]{2,1,0:T(8,128)(2,1)}), (bf16[1,336,4096]{2,1,0:T(8,128)(2,1)}, bf16[1,336,4096]{2,1,0:T(8,128)(2,1)}, ...) | async-done | bytes 8257552 | tf_op jit(solution)/shard_map/psum | solution.py:66
  513.1 3.8 copy.15
  516.9 1.5 copy.16
  518.4 1.2 copy-done.2
  519.7 1.5 copy.17
  521.2 1.0 copy-done.7
  522.2 1.3 copy.18
  (31 shorter events, 0.2 us)
Async XLA Ops:
  7.2 154.9 %copy-start = (bf16[1,336,4096]{2,1,0:T(8,128)(2,1)S(1)}, bf16[1,336,4096]{2,1,0:T(8,128)(2,1)}, u32[]{:S(2)}) copy-start(bf16[1,336,4096]{2,1,0:T(8,128)(2,1)} %param.11) | copy-start | bytes 8257540
  7.2 154.9 %all-gather.2.cloned.1.call-start = ((), (), s32[]{:S(2)}) async-start(), calls=%async_computation.2 | async-start | bytes 8912896 | tf_op jit(solution)/shard_map/all_gather | solution.py:44
  18.1 155.7 %all-to-all-start = ((bf16[16,64,4096]{2,1,0:T(8,128)(2,1)}), bf16[16,64,4096]{2,1,0:T(8,128)(2,1)}, u32[]{:S(2)}, u32[]{:S(2)}) async-start(bf16[16,64,4096]{2,1,0:T(8,128)(2,1)} %stack.2), calls=%async_computation | async-start | bytes 16777216 | tf_op jit(solution)/shard_map/all_to_all | solution.py:46
  25.9 279.0 %reduce-scatter.2.cloned.1.call-start = ((), (), s32[]{:S(2)}) async-start(), calls=%async_computation.3 | async-start | bytes 8912896 | tf_op jit(solution)/shard_map/reduce_scatter | solution.py:70
  162.1 7.6 %copy-start.4 = (bf16[1,336,4096]{2,1,0:T(8,128)(2,1)S(1)}, bf16[1,336,4096]{2,1,0:T(8,128)(2,1)}, u32[]{:S(2)}) copy-start(bf16[1,336,4096]{2,1,0:T(8,128)(2,1)} %param.12) | copy-start | bytes 8257540
  162.1 7.6 %copy-start.10 = (bf16[1024,4096]{1,0:T(8,128)(2,1)S(1)}, bf16[1024,4096]{1,0:T(8,128)(2,1)}, u32[]{:S(2)}) copy-start(bf16[1024,4096]{1,0:T(8,128)(2,1)} %all-gather.2.cloned.1.call-done) | copy-start | bytes 25165828
  182.2 8.4 %copy-start.8 = (bf16[1024,336]{0,1:T(8,128)(2,1)}, bf16[1024,336]{0,1:T(8,128)(2,1)S(1)}, u32[]{:S(2)}) copy-start(bf16[1024,336]{0,1:T(8,128)(2,1)S(1)} %get-tuple-element.10) | copy-start | bytes 2064388
  182.2 8.4 %copy-start.5 = (bf16[1,336,4096]{2,1,0:T(8,128)(2,1)S(1)}, bf16[1,336,4096]{2,1,0:T(8,128)(2,1)}, u32[]{:S(2)}) copy-start(bf16[1,336,4096]{2,1,0:T(8,128)(2,1)} %param.12) | copy-start | bytes 8257540
  200.9 7.8 %copy-start.9 = (bf16[1024,336]{0,1:T(8,128)(2,1)S(1)}, bf16[1024,336]{0,1:T(8,128)(2,1)}, u32[]{:S(2)}) copy-start(bf16[1024,336]{0,1:T(8,128)(2,1)} %copy-done.8) | copy-start | bytes 2064388
  200.9 312.2 %all-reduce.3.cloned.1.call-start = ((), (), s32[]{:S(2)}) async-start(), calls=%async_computation.4 | async-start | bytes 16515072 | tf_op jit(solution)/shard_map/psum | solution.py:66
  208.7 7.8 %copy-start.11 = (f32[1024,336]{0,1:T(8,128)S(1)}, f32[1024,336]{0,1:T(8,128)}, u32[]{:S(2)}) copy-start(f32[1024,336]{0,1:T(8,128)} %fusion.7) | copy-start | bytes 4128772
  208.7 7.8 %copy-start.12 = (f32[1024,336]{0,1:T(8,128)S(1)}, f32[1024,336]{0,1:T(8,128)}, u32[]{:S(2)}) copy-start(f32[1024,336]{0,1:T(8,128)} %fusion.10) | copy-start | bytes 4128772
  306.6 46.5 %collective-permute-start = (bf16[1,1,256,4096]{3,2,1,0:T(8,128)(2,1)S(1)}, bf16[1,1,256,4096]{3,2,1,0:T(8,128)(2,1)S(1)}, u32[]{:S(2)}, u32[]{:S(2)}) collective-permute-start(bf16[1,1,256,4096]{3,2,1,0:T(8,128)(2,1)S(1)} %fusion.3), channel_id=1, source_target_pairs={{16,0},{32,16},{48,32},{17,1},{33,17},{49,33},{18,2},{34,18},{50,3... | collective-permute-start | bytes 6291464 | tf_op jit(solution)/shard_map/ppermute | solution.py:12
  353.2 159.9 %copy-start.6 = (bf16[1,1,256,4096]{3,2,1,0:T(8,128)(2,1)}, bf16[1,1,256,4096]{3,2,1,0:T(8,128)(2,1)S(1)}, u32[]{:S(2)}) copy-start(bf16[1,1,256,4096]{3,2,1,0:T(8,128)(2,1)S(1)} %collective-permute-done) | copy-start | bytes 6291460
  513.1 3.8 copy-start.3
  516.9 2.8 copy-start.2
  519.7 2.6 copy-start.7
  519.7 3.9 copy-start.1
Sparse Core Ops, SparseCore 0:
  11.8 150.2 all-gather.1
  201.1 103.7 reduce-scatter.1
  308.3 204.7 all-reduce.2
